TPU v7x, 256 devices: a whole 4x4x8 slice. The times are simulated.
256 devices in a mesh: inp: 4 (over y_hi, core), dep: 8 (over x, y_lo), out: 8 (over z).
Axes of the slice: x: 4, y: 4 (y_hi: 2, y_lo: 2; y = y_hi * 2 + y_lo), z: 8, core: 2. Of those that a mesh axis runs over, the one named last changes fastest.
Arguments:
- tokens: bfloat16 [1024, 16384], P('inp', 'out'), may hold values from -6 to 6
- gate_up_weight: bfloat16 [16384, 2, 28672], P('out', None, ('inp', 'dep')), may hold values from -0.046875 to 0.046875
- down_weight: bfloat16 [28672, 16384], P(('inp', 'dep'), 'out'), may hold values from -0.03125 to 0.03125
Outputs:
- layer_output: bfloat16 [1024, 16384], P(('inp', 'dep'), 'out')
All inputs are finite; a program needn't handle non-finite values.
Results may differ from a plain program's by a relative error of at most 0.0049.
Values may be sent and summed in bfloat16 or wider, within the bound.
A program may use at most 128 MiB of HBM per device.

v0:
```python
import jax
import jax.numpy as jnp
from jax import lax
from jax.sharding import PartitionSpec as P


def swiglu(projected):
    return (jax.nn.silu(projected[:, 0, :]) * projected[:, 1, :]).astype(jnp.bfloat16)


def shards(tokens, gate_up_weight, down_weight):
    local_width = gate_up_weight.shape[0]
    block_units = gate_up_weight.shape[2]
    flat_weight = gate_up_weight.reshape(local_width, 2 * block_units)
    projected = jnp.dot(
        lax.all_gather(tokens, "inp", axis=0, tiled=True),
        flat_weight,
        preferred_element_type=jnp.float32,
    )
    projected = projected.reshape(projected.shape[0], 2, block_units)
    totals = lax.psum(projected, "out")
    full_hidden = swiglu(totals)
    result = lax.psum_scatter(
        jnp.dot(full_hidden, down_weight, preferred_element_type=jnp.float32),
        ("inp", "dep"),
        scatter_dimension=0,
        tiled=True,
    )
    return result.astype(jnp.bfloat16)


def solution(mesh):
    placed = (P("inp", "out"), P("out", None, ("inp", "dep")), P(("inp", "dep"), "out"))
    return jax.shard_map(
        shards, mesh=mesh, in_specs=placed, out_specs=P(("inp", "dep"), "out"), check_vma=False
    )
```

profile of v0, /device:TPU:1, one launch (start us, length us, event | category | flops | bytes accessed | tf_op | source)
XLA Modules:
  0.0 441.7 jit_solution(10383628695858579418)
XLA Ops:
  6.5 0.0 all-gather.2.cloned.1.call-start
  6.5 0.7 all-gather.2.cloned.1.call-update
  7.3 0.0 all-reduce.2.cloned.1.call-start
  7.3 7.6 %copy.5 = bf16[256,8,2,896]{3,1,2,0:T(8,128)(2,1)} copy(bf16[256,8,2,896]{3,2,1,0:T(2,128)(2,1)} %bitcast.23) | data formatting | bytes 14680064
  14.9 10.5 %copy.4 = bf16[1792,2048]{1,0:T(8,128)(2,1)} copy(bf16[1792,2048]{0,1:T(8,128)(2,1)} %bitcast.22) | data formatting | bytes 14680064 | tf_op jit(solution)/shard_map/dot_general | solution.py:15
  25.4 29.1 %all-gather.2.cloned.1.call-done = bf16[1024,2048]{1,0:T(8,128)(2,1)} async-done(((bf16[256,2048]{1,0:T(8,128)(2,1)}), bf16[1024,2048]{1,0:T(8,128)(2,1)}) %all-gather.2.cloned.1.call-update) | async-done | bytes 4194320 | tf_op jit(solution)/shard_map/all_gather | solution.py:16
  54.5 14.3 %fusion = f32[1024,2,896]{2,0,1:T(8,128)} fusion(bf16[2,896,2048]{2,1,0:T(8,128)(2,1)} %bitcast.24, bf16[1024,2048]{1,0:T(8,128)(2,1)} %all-gather.2.cloned.1.call-done), kind=kOutput, calls=%fused_computation | convolution fusion | flops 7516192768 | bytes 18874368 | tf_op jit(solution)/shard_map/dot_general | solution.py:15
  68.8 0.0 all-reduce.2.cloned.1.call-update
  68.8 0.0 reduce-scatter.2.cloned.1.call-start
  68.9 167.4 %all-reduce.2.cloned.1.call-done = f32[1024,2,896]{2,0,1:T(8,128)} async-done(((f32[1024,2,896]{2,0,1:T(8,128)}), f32[1024,2,896]{2,0,1:T(8,128)}) %all-reduce.2.cloned.1.call-update) | async-done | bytes 7340048 | tf_op jit(solution)/shard_map/psum | solution.py:21
  236.3 11.9 %fusion.4 = f32[1024,2048]{1,0:T(8,128)} fusion(bf16[896,2048]{1,0:T(8,128)(2,1)} %param.5, f32[1024,2,896]{2,0,1:T(8,128)} %all-reduce.2.cloned.1.call-done), kind=kOutput, calls=%fused_computation.6 | convolution fusion | flops 3763601408 | bytes 19398656 | tf_op jit(solution)/shard_map/dot_general | solution.py:24
  248.2 0.0 reduce-scatter.2.cloned.1.call-update
  248.2 185.4 %reduce-scatter.2.cloned.1.call-done = f32[32,2048]{1,0:T(8,128)} async-done(((f32[1024,2048]{1,0:T(8,128)}), f32[32,2048]{1,0:T(8,128)}) %reduce-scatter.2.cloned.1.call-update) | async-done | bytes 262160 | tf_op jit(solution)/shard_map/reduce_scatter | solution.py:23
  433.6 1.6 convert_element_type.7
Async XLA Ops:
  6.5 48.0 %all-gather.2.cloned.1.call-start = ((), (), s32[]{:S(2)}) async-start(), calls=%async_computation.1 | async-start | bytes 5242880 | tf_op jit(solution)/shard_map/all_gather | solution.py:16
  7.3 229.0 %all-reduce.2.cloned.1.call-start = ((), (), s32[]{:S(2)}) async-start(), calls=%async_computation.2 | async-start | bytes 14680064 | tf_op jit(solution)/shard_map/psum | solution.py:21
  68.8 364.8 %reduce-scatter.2.cloned.1.call-start = ((), (), s32[]{:S(2)}) async-start(), calls=%async_computation.3 | async-start | bytes 8650752 | tf_op jit(solution)/shard_map/reduce_scatter | solution.py:23
Sparse Core Ops, SparseCore 0:
  9.2 45.2 all-gather.1
  68.9 167.2 all-reduce.1
  248.3 185.1 reduce-scatter.1
where the time goes:
time: 444 us; the launch traced here: 442 us
  waiting for transfers between devices  383 us (86%)
  matrix products  26.2 us (6%)
  local copies, waits for them, and re-layouts  18.1 us (4%)
  between operations  13.1 us (3%)
    reduce_scatter x1, waiting for transfers between devices, shards(): lax.psum_scatter(jnp.dot(full_hidden, down_weight, preferred_element_type...  185 us
    psum x1, waiting for transfers between devices, shards(): totals = lax.psum(projected, 'out')  167 us
    all_gather x1, waiting for transfers between devices, shards(): lax.all_gather(tokens, 'inp', axis=0, tiled=True)  29.1 us
    dot_general x1, matrix products, shards(): jnp.dot(lax.all_gather(tokens, 'inp', axis=0, tiled=True), flat_weight, p...  14.3 us
    dot_general x1, matrix products, shards(): jnp.dot(full_hidden, down_weight, preferred_element_type=jnp.float32)  11.9 us
    dot_general x1, local copies, waits for them, and re-layouts, shards(): jnp.dot(lax.all_gather(tokens, 'inp', axis=0, tiled=True), flat_weight, p...  10.5 us
  transfers between devices with their start and end apart: 3, of which 3 were waited for; matrix products, arithmetic and copies ran while one was open for 4% of the time, Pallas kernels for 0%

commit v1 on v0

v1 whole, which is shorter than its diff:
```python
import jax
import jax.numpy as jnp
from jax import lax
from jax.experimental import pallas as pl
from jax.experimental.pallas import tpu as pltpu
from jax.sharding import PartitionSpec as P

MESH = pl.DeviceIdType.MESH
BF16, F32 = jnp.bfloat16, jnp.float32
UNITS, NZ, NX, ROWS = 4, 8, 4, 32
LANES = 128
START = (0, 4, 7, 10)


def encode(v):
    return (v * jnp.abs(v)).astype(BF16)


def decode(v):
    v = v.astype(F32)
    root = jnp.sqrt(jnp.abs(v))
    return jnp.where(v < 0, -root, root)


def kernel(
    tok, gate_up, down, out,
    X, raw, flat, W, D, PS, SA, SB, RA, RB, HA, HB, own, pair_out, pair_in, xs, xr, ys, yr,
    ld_sem, w_sem, tk_s, tk_r, rs_s, rs_r, ag_s, ag_r, pr_s, pr_r, x_s, x_r, y_s, y_r,
):
    inp, dep, z = lax.axis_index("inp"), lax.axis_index("dep"), lax.axis_index("out")
    x, l = dep // 2, lax.rem(dep, 2)
    h, c = inp // 2, lax.rem(inp, 2)
    dep_l = x * 2 + (1 - l)
    partner = (h * 2 + (1 - c), dep, z)
    y_near = (inp, dep_l, z)
    y_far = ((1 - h) * 2 + c, dep, z)
    cross = ((1 - h) * 2 + c, dep_l, z)
    x_next = (inp, lax.rem(dep + 2, 8), z)
    x_prev = (inp, lax.rem(dep + 6, 8), z)
    z_next = (inp, dep, lax.rem(z + 1, NZ))
    z_prev = (inp, dep, lax.rem(z + NZ - 1, NZ))
    unit_half = ((0, 1 - l), (1, l), (1, 1 - l), (0, l))
    unit_target = (y_near, y_far, cross)

    blocks_a = SA.shape[-1] // (2 * LANES)
    blocks = raw.shape[0]
    wide = (SA.shape[-1], SB.shape[-1])
    first = (0, SA.shape[-1])
    sends = (SA, SB)
    receives = (RA, RB)
    hidden = (HA, HB)
    started = []

    def weight_copy(j):
        columns = pl.ds(pl.multiple_of(j * LANES, LANES), LANES)
        return pltpu.make_async_copy(gate_up.at[:, :, columns], raw.at[j], w_sem.at[j])

    def own_copy(q):
        lp = (1 - l) if q == 0 else l
        return pltpu.make_async_copy(tok.at[:, lp], X.at[0, :, lp], ld_sem.at[q])

    down_copy = pltpu.make_async_copy(down, D, ld_sem.at[2])

    def remote(src, dst, s, r, device):
        return pltpu.make_async_remote_copy(
            src_ref=src, dst_ref=dst, send_sem=s, recv_sem=r, device_id=device, device_id_type=MESH
        )

    def go(copy):
        copy.start()
        started.append(copy)

    own_copy(0).start()
    for j in range(blocks):
        weight_copy(j).start()
    own_copy(1).start()
    down_copy.start()

    barrier = pltpu.get_barrier_semaphore()
    peers = (partner, y_near, y_far, cross, x_next, x_prev, z_next, z_prev)
    for peer in peers:
        pl.semaphore_signal(barrier, inc=1, device_id=peer, device_id_type=MESH)
    pl.semaphore_wait(barrier, len(peers))

    def tok_pair(q):
        lp = (1 - l) if q == 0 else l
        return remote(tok.at[:, lp], X.at[1, :, lp], tk_s.at[q], tk_r.at[q], partner)

    def tok_cross(p):
        return remote(tok.at[p, 1 - l], X.at[2, p, 1 - l], tk_s.at[2 + p], tk_r.at[2 + p], cross)

    def tok_cross_in(p):
        return remote(X.at[2, p, l], X.at[2, p, l], tk_s.at[2 + p], tk_r.at[2 + p], cross)

    def tok_relay(p):
        return remote(X.at[2, p, l], X.at[2, p, l], tk_s.at[6 + p], tk_r.at[6 + p], y_near)

    def tok_relay_in(p):
        return remote(X.at[2, p, 1 - l], X.at[2, p, 1 - l], tk_s.at[6 + p], tk_r.at[6 + p], y_near)

    def tok_forward(q, p):
        lp = l if q == 0 else 1 - l
        i = 10 + 4 * q + p
        return remote(X.at[2, p, lp], X.at[3, p, lp], tk_s.at[i], tk_r.at[i], partner)

    def tok_forward_in(q, p):
        lp = l if q == 0 else 1 - l
        i = 10 + 4 * q + p
        return remote(X.at[3, p, lp], X.at[3, p, lp], tk_s.at[i], tk_r.at[i], partner)

    go(tok_pair(0))
    for p in range(NX):
        go(tok_cross(p))
    go(tok_pair(1))

    def cross_piece(p):
        tok_cross_in(p).wait_recv()
        go(tok_relay(p))
        go(tok_forward(0, p))

    def relay_piece(p):
        tok_relay_in(p).wait_recv()
        go(tok_forward(1, p))

    def flatten(j):
        weight_copy(j).wait()
        depth = flat.shape[0] // 2

        def part(i, carry):
            k = pl.multiple_of(i * depth, depth)
            flat[...] = raw[j, pl.ds(k, depth)].reshape(2 * depth, LANES).astype(F32)
            W[j, pl.ds(k, depth), 0:LANES] = flat[pl.ds(0, depth, stride=2), :].astype(BF16)
            W[j, pl.ds(k, depth), LANES:] = flat[pl.ds(1, depth, stride=2), :].astype(BF16)
            return carry

        lax.fori_loop(0, W.shape[1] // depth, part, 0)

    def project(u, j0, j1):
        hb, lp = unit_half[u]

        def block(j, carry):
            if u == 0:
                flatten(j)
            rows = X[2 * hb:2 * hb + 2, :, lp].reshape(NZ * ROWS, X.shape[-1])
            sums = jnp.dot(rows, W[j], preferred_element_type=F32)
            columns = pl.ds(pl.multiple_of(j * 2 * LANES, 2 * LANES), 2 * LANES)
            PS[u, :, :, columns] = sums.reshape(NZ, ROWS, 2 * LANES)
            return carry

        lax.fori_loop(j0, j1, block, 0)

    def hops(g, d):
        return 4 if g == d else 3

    def slot(g, d, k):
        return k if g == d else 4 + k

    def z_copy(u, g, d, k):
        i = 7 * g + slot(g, d, k)
        ref = slot(g, d, k)
        return remote(
            sends[g].at[u, ref], receives[g].at[u, ref], rs_s.at[u, i], rs_r.at[u, i], z_next if d == 0 else z_prev
        )

    def step(d, k):
        return k if d == 0 else -k

    def sum_send(u, g, d, k):
        n = hops(g, d)
        o = lax.rem(z + step(d, n - k) + NZ, NZ)
        v = PS[u, o, :, first[g]:first[g] + wide[g]]
        if k > 0:
            z_copy(u, g, d, k - 1).wait_recv()
            v = v + decode(receives[g][u, slot(g, d, k - 1)])
        sends[g][u, slot(g, d, k)] = encode(v)
        go(z_copy(u, g, d, k))

    def sum_last(u, g):
        for d in (0, 1):
            z_copy(u, g, d, hops(g, d) - 1).wait_recv()
        v = PS[u, z, :, first[g]:first[g] + wide[g]]
        for d in (0, 1):
            v = v + decode(receives[g][u, slot(g, d, hops(g, d) - 1)])
        for b in range(wide[g] // (2 * LANES)):
            gate = v[:, 2 * b * LANES:(2 * b + 1) * LANES]
            up = v[:, (2 * b + 1) * LANES:(2 * b + 2) * LANES]
            hidden[g][u, z, :, b * LANES:(b + 1) * LANES] = (gate / (1 + jnp.exp(-gate)) * up).astype(BF16)

    def h_copy(u, g, d, k, o):
        i = 7 * g + slot(g, d, k)
        ref = hidden[g].at[u, o]
        return remote(ref, ref, ag_s.at[u, i], ag_r.at[u, i], z_next if d == 0 else z_prev)

    def h_wait(u, g, d, k):
        h_copy(u, g, d, k, lax.rem(z - step(d, k + 1) + NZ, NZ)).wait_recv()

    def h_send(u, g, d, k):
        if k > 0:
            h_wait(u, g, d, k - 1)
        go(h_copy(u, g, d, k, lax.rem(z - step(d, k) + NZ, NZ)))

    half = own.shape[-1]

    def pair_copy(u, b):
        return remote(pair_out.at[u, b], pair_in.at[u, b], pr_s.at[u, b], pr_r.at[u, b], partner)

    def project_down(u, b):
        ka = HA.shape[-1]

        def block(i, carry):
            at = pl.multiple_of(i * 2 * LANES, 2 * LANES)
            columns = pl.ds(b * half + at, 2 * LANES)
            v = jnp.dot(HA[u].reshape(NZ * ROWS, ka), D[0:ka, columns], preferred_element_type=F32)
            v = v + jnp.dot(
                HB[u].reshape(NZ * ROWS, HB.shape[-1]), D[ka:, columns], preferred_element_type=F32
            )
            v = v.reshape(2, NX, ROWS, 2 * LANES)
            own[u % 2, b, :, :, pl.ds(at, 2 * LANES)] = v[0]
            pair_out[u, b, :, :, pl.ds(at, 2 * LANES)] = v[1].astype(BF16)
            return carry

        lax.fori_loop(0, half // (2 * LANES), block, 0)
        go(pair_copy(u, b))

    def x_copy(u, i):
        return remote(xs.at[u, i], xr.at[u, i], x_s.at[u, i], x_r.at[u, i], x_next if i < 3 else x_prev)

    def piece(u, b, k):
        p = lax.rem(x + k + NX, NX)
        return own[u % 2, b, p] + pair_in[u, b, p].astype(F32)

    def x_first(u):
        for b in (0, 1):
            pair_copy(u, b).wait_recv()
            i = 3 * b
            xs[u, i] = piece(u, b, 2).astype(BF16)
            go(x_copy(u, i))
            i = 4 if b == 0 else 1
            xs[u, i] = piece(u, b, -1 if b == 0 else 1).astype(BF16)
            go(x_copy(u, i))

    def x_second(u):
        for b in (0, 1):
            i = 3 * b
            x_copy(u, i).wait_recv()
            xs[u, i + 2] = (piece(u, b, 1 if b == 0 else -1) + xr[u, i].astype(F32)).astype(BF16)
            go(x_copy(u, i + 2))

    def y_copy(u, b):
        return remote(ys.at[u, b], yr.at[u, b], y_s.at[u, b], y_r.at[u, b], unit_target[u])

    def x_last(u):
        for b in (0, 1):
            two, one = 3 * b + 2, (4 if b == 0 else 1)
            x_copy(u, one).wait_recv()
            x_copy(u, two).wait_recv()
            v = piece(u, b, 0) + xr[u, one].astype(F32) + xr[u, two].astype(F32)
            if u < UNITS - 1:
                ys[u, b] = v.astype(BF16)
                go(y_copy(u, b))
            else:
                for other in range(UNITS - 1):
                    y_copy(other, b).wait_recv()
                    v = v + yr[other, b].astype(F32)
                out[:, b * half:(b + 1) * half] = v.astype(BF16)

    order = ((0, 0), (1, 1), (0, 1), (1, 0))
    own_copy(0).wait()
    tok_pair(0).wait_recv()
    for tick in range(START[-1] + 12):
        for u in range(UNITS):
            k = tick - START[u]
            if k == 0:
                for g, j0, j1 in ((0, 0, blocks_a), (1, blocks_a, blocks)):
                    if u == 0:
                        project(u, j0, j1)
                    for d in (0, 1):
                        sum_send(u, g, d, 0)
        for u in range(UNITS):
            k = tick - START[u]
            if 5 <= k < 8:
                for g, d in order:
                    if k - 4 < hops(g, d):
                        h_send(u, g, d, k - 4)
            if 1 <= k < 4:
                for g, d in order:
                    if k < hops(g, d):
                        sum_send(u, g, d, k)
            if k == 4:
                for g in (0, 1):
                    sum_last(u, g)
                    for d in (0, 1):
                        h_send(u, g, d, 0)
            if k == 8:
                if u == 0:
                    down_copy.wait()
                for g, d in order:
                    h_wait(u, g, d, hops(g, d) - 1)
                for b in (0, 1):
                    project_down(u, b)
            if k == 9:
                x_first(u)
            if k == 10:
                x_second(u)
            if k == 11:
                x_last(u)
        if tick < 2:
            cross_piece(tick)
        elif tick == 2:
            cross_piece(2)
            cross_piece(3)
        elif tick == 3:
            for p in range(NX):
                tok_forward_in(0, p).wait_recv()
            project(1, 0, blocks)
            for p in range(NX):
                relay_piece(p)
        elif tick == 4:
            for p in range(NX):
                tok_forward_in(1, p).wait_recv()
        if 4 <= tick < 7:
            project(2, (0, 3, 5)[tick - 4], (3, 5, 7)[tick - 4])
        if tick == 7:
            own_copy(1).wait()
            tok_pair(1).wait_recv()
        if 7 <= tick < 10:
            project(3, (0, 3, 5)[tick - 7], (3, 5, 7)[tick - 7])

    for copy in started:
        copy.wait_send()


def shards(tokens, gate_up_weight, down_weight):
    width = tokens.shape[1]
    units = gate_up_weight.shape[2]
    blocks = units // LANES
    ua = (blocks + 1) // 2 * LANES
    ub = units - ua
    half = width // 2
    dma = pltpu.SemaphoreType.DMA
    any_space = pl.BlockSpec(memory_space=pl.ANY)
    vmem = pltpu.VMEM
    return pl.pallas_call(
        kernel,
        out_shape=jax.ShapeDtypeStruct((ROWS, width), BF16),
        in_specs=[any_space] * 3,
        out_specs=pl.BlockSpec(memory_space=pltpu.VMEM),
        scratch_shapes=[
            vmem((4, NX, 2, ROWS, width), BF16),
            vmem((blocks, width, 2, LANES), BF16),
            vmem((512, LANES), F32),
            vmem((blocks, width, 2 * LANES), BF16),
            vmem((units, width), BF16),
            vmem((UNITS, NZ, ROWS, 2 * units), F32),
            vmem((UNITS, 7, ROWS, 2 * ua), BF16),
            vmem((UNITS, 7, ROWS, 2 * ub), BF16),
            vmem((UNITS, 7, ROWS, 2 * ua), BF16),
            vmem((UNITS, 7, ROWS, 2 * ub), BF16),
            vmem((UNITS, NZ, ROWS, ua), BF16),
            vmem((UNITS, NZ, ROWS, ub), BF16),
            vmem((2, 2, NX, ROWS, half), F32),
            vmem((UNITS, 2, NX, ROWS, half), BF16),
            vmem((UNITS, 2, NX, ROWS, half), BF16),
            vmem((UNITS, 6, ROWS, half), BF16),
            vmem((UNITS, 6, ROWS, half), BF16),
            vmem((UNITS - 1, 2, ROWS, half), BF16),
            vmem((UNITS - 1, 2, ROWS, half), BF16),
            dma((3,)),
            dma((blocks,)),
            dma((18,)),
            dma((18,)),
            dma((UNITS, 14)),
            dma((UNITS, 14)),
            dma((UNITS, 14)),
            dma((UNITS, 14)),
            dma((UNITS, 2)),
            dma((UNITS, 2)),
            dma((UNITS, 6)),
            dma((UNITS, 6)),
            dma((UNITS - 1, 2)),
            dma((UNITS - 1, 2)),
        ],
        compiler_params=pltpu.CompilerParams(
            collective_id=0, has_side_effects=True, vmem_limit_bytes=62 << 20
        ),
    )(tokens.reshape(NX, 2, ROWS, width), gate_up_weight, down_weight)


def solution(mesh):
    placed = (P("inp", "out"), P("out", None, ("inp", "dep")), P(("inp", "dep"), "out"))
    return jax.shard_map(
        shards, mesh=mesh, in_specs=placed, out_specs=P(("inp", "dep"), "out"), check_vma=False
    )
```

time: 444 us -> 112 us (0.25)
  waiting for transfers between devices: 383 us -> 0 us
  Pallas kernels: 0 us -> 111 us
  matrix products: 26.2 us -> 0 us
  local copies, waits for them, and re-layouts: 18.1 us -> 1.57 us
  between operations: 13.1 us -> 0.01 us
    reduce_scatter x1 -> x0, waiting for transfers between devices: 185 us -> none  [shards(): lax.psum_scatter(jnp.dot(full_hidden, down_weight, preferred_element_type...]
    psum x1 -> x0, waiting for transfers between devices: 167 us -> none  [shards(): totals = lax.psum(projected, 'out')]
    pallas_call x0 -> x1, Pallas kernels: none -> 111 us  [shards(): pl.pallas_call(kernel, out_shape=jax.ShapeDtypeStruct((ROWS, width), BF16...]
    all_gather x1 -> x0, waiting for transfers between devices: 29.1 us -> none  [shards(): lax.all_gather(tokens, 'inp', axis=0, tiled=True)]
    dot_general x2 -> x0, matrix products: 26.2 us -> none  [the longest x1 14.3 us: shards(): jnp.dot(lax.all_gather(tokens, 'inp', axis=0, tiled=True), flat_weight, p...]
    dot_general x1 -> x0, local copies, waits for them, and re-layouts: 10.5 us -> none  [shards(): jnp.dot(lax.all_gather(tokens, 'inp', axis=0, tiled=True), flat_weight, p...]
    unnamed x1, local copies, waits for them, and re-layouts: 7.6 us -> 1.57 us
  transfers between devices with their start and end apart: 3 -> 0, of which waited for: 3 -> 0; matrix products, arithmetic and copies ran while one was open for 4% -> 0% of each run, Pallas kernels for 0% -> 0%
where the time goes in v1:
time: 112 us
  Pallas kernels  111 us (99%)
  local copies, waits for them, and re-layouts  1.57 us (1%)
    pallas_call x1, Pallas kernels, shards(): pl.pallas_call(kernel, out_shape=jax.ShapeDtypeStruct((ROWS, width), BF16...  111 us

profile of v1, /device:TPU:1, one launch (start us, length us, event | category | flops | bytes accessed | tf_op | source)
XLA Modules:
  0.0 112.2 jit_solution(16057753182893407074)
XLA Ops:
  0.0 110.7 %shard_map.37 = bf16[32,2048]{1,0:T(8,128)(2,1)} custom-call(bf16[4,2,32,2048]{3,2,1,0:T(8,128)(2,1)} %bitcast.1, bf16[2048,2,896]{2,1,0:T(2,128)(2,1)} %gate_up.1, bf16[896,2048]{1,0:T(8,128)(2,1)} %down.1), custom_call_target="tpu_custom_call" | custom-call | tf_op jit(solution)/shard_map/pallas_call | solution.py:343
  110.7 1.6 %copy.5 = bf16[32,2048]{1,0:T(8,128)(2,1)} copy(bf16[32,2048]{1,0:T(8,128)(2,1)} %shard_map.37) | data formatting | bytes 262144

commit v2 on v0

v2 whole, which is shorter than its diff:
```python
import jax
import jax.numpy as jnp
from jax import lax
from jax.experimental import pallas as pl
from jax.experimental.pallas import tpu as pltpu
from jax.sharding import PartitionSpec as P

MESH = pl.DeviceIdType.MESH
BF16, F32 = jnp.bfloat16, jnp.float32
UNITS, NZ, NX, ROWS = 4, 8, 4, 32
LANES = 128
GROUPS = (4, 3)
STAGES = ((0, 0, 32), (1, 0, 32), (2, 0, 32), (3, 0, 32))
PARTS = 4
LONG = ((False, False), (False, False), (False, False), (False, True))
CROSS, RELAY, WEIGHT, PRODUCT, SUM, END, HIDDEN, DOWN, X1, X2, X3 = range(11)
ORDER = (
    (WEIGHT, 0), (WEIGHT, 1), (WEIGHT, 2), (WEIGHT, 3), (PRODUCT, 3, 0), (PRODUCT, 3, 1), (PRODUCT, 3, 2), (PRODUCT, 3, 3),
    (SUM, 3, 0, 0, 0), (SUM, 3, 0, 1, 0), (PRODUCT, 0, 0), (PRODUCT, 0, 1), (PRODUCT, 0, 2), (PRODUCT, 0, 3),
    (SUM, 0, 0, 1, 0), (SUM, 0, 0, 0, 0), (WEIGHT, 4), (PRODUCT, 0, 4), (CROSS, 0), (CROSS, 1), (WEIGHT, 5),
    (SUM, 3, 0, 0, 1), (PRODUCT, 0, 5), (WEIGHT, 6), (PRODUCT, 0, 6), (SUM, 0, 1, 0, 0), (SUM, 0, 1, 1, 0),
    (SUM, 0, 0, 1, 1), (CROSS, 2), (SUM, 0, 0, 0, 1), (PRODUCT, 3, 4), (PRODUCT, 3, 5), (PRODUCT, 3, 6), (SUM, 3, 0, 1, 1),
    (SUM, 3, 1, 0, 0), (CROSS, 3), (SUM, 3, 1, 1, 0), (PRODUCT, 1, 0), (SUM, 3, 0, 0, 2), (PRODUCT, 1, 1), (PRODUCT, 1, 2),
    (PRODUCT, 1, 3), (SUM, 1, 0, 0, 0), (SUM, 0, 1, 1, 1), (SUM, 1, 0, 1, 0), (RELAY, 0), (RELAY, 1), (RELAY, 2),
    (SUM, 0, 0, 0, 2), (SUM, 0, 0, 1, 2), (SUM, 0, 1, 0, 1), (PRODUCT, 1, 4), (PRODUCT, 1, 5), (PRODUCT, 1, 6),
    (SUM, 1, 1, 1, 0), (SUM, 1, 1, 0, 0), (RELAY, 3), (SUM, 3, 1, 0, 1), (SUM, 3, 1, 1, 1), (PRODUCT, 2, 0),
    (PRODUCT, 2, 1), (SUM, 1, 0, 0, 1), (SUM, 0, 1, 1, 2), (PRODUCT, 2, 2), (SUM, 1, 0, 1, 1), (SUM, 0, 0, 0, 3),
    (PRODUCT, 2, 3), (SUM, 2, 0, 0, 0), (SUM, 0, 1, 0, 2), (SUM, 1, 1, 1, 1), (PRODUCT, 2, 4), (SUM, 2, 0, 1, 0),
    (SUM, 1, 1, 0, 1), (PRODUCT, 2, 5), (PRODUCT, 2, 6), (SUM, 2, 1, 1, 0), (SUM, 2, 1, 0, 0), (SUM, 1, 0, 0, 2),
    (SUM, 0, 1, 1, 3), (SUM, 1, 1, 1, 2), (END, 0, 0), (HIDDEN, 0, 0, 1, 0), (HIDDEN, 0, 0, 0, 0), (SUM, 2, 0, 0, 1),
    (SUM, 2, 0, 1, 1), (SUM, 2, 1, 1, 1), (SUM, 1, 1, 0, 2), (END, 0, 1), (HIDDEN, 0, 1, 1, 0), (SUM, 2, 1, 0, 1),
    (SUM, 1, 1, 1, 3), (SUM, 1, 0, 1, 2), (SUM, 1, 0, 0, 3), (SUM, 3, 1, 1, 2), (SUM, 2, 0, 0, 2), (HIDDEN, 0, 1, 0, 0),
    (SUM, 2, 1, 1, 2), (HIDDEN, 0, 1, 1, 1), (HIDDEN, 0, 0, 1, 1), (HIDDEN, 0, 0, 0, 1), (SUM, 2, 1, 0, 2), (END, 1, 1),
    (HIDDEN, 1, 1, 1, 0), (HIDDEN, 1, 1, 0, 0), (SUM, 2, 0, 1, 2), (END, 1, 0), (HIDDEN, 1, 0, 0, 0), (HIDDEN, 1, 0, 1, 0),
    (SUM, 2, 0, 0, 3), (SUM, 2, 1, 1, 3), (HIDDEN, 0, 1, 0, 1), (HIDDEN, 0, 0, 0, 2), (HIDDEN, 0, 1, 1, 2),
    (SUM, 3, 1, 0, 2), (HIDDEN, 1, 1, 1, 1), (SUM, 3, 0, 1, 2), (SUM, 3, 1, 1, 3), (HIDDEN, 1, 0, 0, 1), (SUM, 3, 0, 0, 3),
    (HIDDEN, 1, 0, 1, 1), (END, 2, 0), (HIDDEN, 2, 0, 0, 0), (HIDDEN, 1, 1, 0, 1), (END, 2, 1), (HIDDEN, 2, 1, 1, 0),
    (HIDDEN, 0, 1, 0, 2), (HIDDEN, 1, 1, 1, 2), (HIDDEN, 0, 1, 1, 3), (HIDDEN, 0, 0, 1, 2), (HIDDEN, 1, 0, 0, 2),
    (HIDDEN, 2, 0, 1, 0), (HIDDEN, 0, 0, 0, 3), (END, 3, 0), (HIDDEN, 2, 1, 0, 0), (HIDDEN, 2, 0, 0, 1),
    (HIDDEN, 3, 0, 0, 0), (HIDDEN, 2, 1, 1, 1), (HIDDEN, 1, 0, 1, 2), (HIDDEN, 1, 1, 0, 2), (HIDDEN, 1, 1, 1, 3),
    (END, 3, 1), (HIDDEN, 3, 1, 1, 1), (HIDDEN, 1, 0, 0, 3), (HIDDEN, 3, 1, 0, 1), (DOWN, 0, 0), (HIDDEN, 2, 1, 0, 1),
    (HIDDEN, 2, 0, 1, 1), (HIDDEN, 3, 1, 1, 0), (DOWN, 0, 1), (HIDDEN, 2, 0, 0, 2), (DOWN, 0, 2), (HIDDEN, 2, 1, 1, 2),
    (HIDDEN, 3, 0, 0, 1), (HIDDEN, 3, 0, 1, 1), (X1, 0, 0), (DOWN, 0, 3), (X1, 0, 1), (DOWN, 1, 0), (X1, 0, 2),
    (DOWN, 1, 1), (HIDDEN, 2, 1, 0, 2), (X1, 0, 3), (HIDDEN, 2, 0, 1, 2), (DOWN, 1, 2), (HIDDEN, 2, 0, 0, 3), (X1, 1, 0),
    (HIDDEN, 2, 1, 1, 3), (HIDDEN, 3, 1, 1, 3), (HIDDEN, 3, 0, 1, 0), (X2, 0, 0), (X1, 1, 1), (HIDDEN, 3, 0, 0, 2),
    (HIDDEN, 3, 1, 0, 0), (HIDDEN, 3, 1, 1, 2), (DOWN, 1, 3), (X2, 0, 1), (X1, 1, 2), (X2, 0, 2), (X2, 0, 3),
    (HIDDEN, 3, 1, 0, 2), (HIDDEN, 3, 0, 0, 3), (X1, 1, 3), (X2, 1, 0), (HIDDEN, 3, 0, 1, 2), (X3, 0, 0), (X2, 1, 1),
    (DOWN, 2, 0), (X3, 0, 1), (DOWN, 2, 1), (X2, 1, 2), (X3, 0, 2), (DOWN, 2, 2), (X1, 2, 0), (X3, 0, 3), (X2, 1, 3),
    (DOWN, 2, 3), (X1, 2, 1), (X3, 1, 0), (DOWN, 3, 0), (X1, 2, 2), (X3, 1, 1), (DOWN, 3, 1), (X1, 2, 3), (X3, 1, 2),
    (DOWN, 3, 2), (X1, 3, 0), (X2, 2, 0), (X3, 1, 3), (X1, 3, 1), (DOWN, 3, 3), (X2, 2, 1), (X1, 3, 2), (X2, 2, 2),
    (X2, 2, 3), (X1, 3, 3), (X2, 3, 1), (X3, 2, 1), (X2, 3, 0), (X3, 2, 0), (X3, 2, 2), (X2, 3, 2), (X3, 2, 3), (X2, 3, 3),
    (X3, 3, 1), (X3, 3, 0), (X3, 3, 2), (X3, 3, 3),
)


def encode(v):
    return (v * jnp.abs(v)).astype(BF16)


def decode(v):
    v = v.astype(F32)
    root = jnp.sqrt(jnp.abs(v))
    return jnp.where(v < 0, -root, root)


def kernel(
    tok, gate_up, down, out,
    X, raw, flat, W, D, PS, S, R, H, own, pair_out, pair_in, xs, xr, ys, yr,
    ld_sem, w_sem, tk_s, tk_r, rs_s, rs_r, ag_s, ag_r, pr_s, pr_r, x_s, x_r, y_s, y_r,
):
    inp, dep, z = lax.axis_index("inp"), lax.axis_index("dep"), lax.axis_index("out")
    x, l = dep // 2, lax.rem(dep, 2)
    h, c = inp // 2, lax.rem(inp, 2)
    dep_l = x * 2 + (1 - l)
    partner = (h * 2 + (1 - c), dep, z)
    y_near = (inp, dep_l, z)
    y_far = ((1 - h) * 2 + c, dep, z)
    cross = ((1 - h) * 2 + c, dep_l, z)
    x_side = ((inp, lax.rem(dep + 2, 8), z), (inp, lax.rem(dep + 6, 8), z))
    reach = 3 if any(a or b for a, b in LONG) else 1
    z_side = tuple((inp, dep, lax.rem(z + k, NZ)) for k in range(1, reach + 1))
    z_side += tuple((inp, dep, lax.rem(z + NZ - k, NZ)) for k in range(1, reach + 1))
    unit_half = ((0, 1 - l), (1, l), (1, 1 - l), (0, l))
    unit_target = (y_near, y_far, cross)
    blocks = raw.shape[0]
    first = [sum(GROUPS[:g]) for g in range(len(GROUPS))]
    part = own.shape[-1]
    started = []

    def weight_copy(j):
        columns = pl.ds(j * LANES, LANES)
        return pltpu.make_async_copy(gate_up.at[:, :, columns], raw.at[j], w_sem.at[j])

    def own_copy(q):
        lp = (1 - l) if q == 0 else l
        return pltpu.make_async_copy(tok.at[:, lp], X.at[0, :, lp], ld_sem.at[q])

    down_copy = pltpu.make_async_copy(down, D, ld_sem.at[2])

    def remote(src, dst, s, r, device):
        return pltpu.make_async_remote_copy(
            src_ref=src, dst_ref=dst, send_sem=s, recv_sem=r, device_id=device, device_id_type=MESH
        )

    def go(copy):
        copy.start()
        started.append(copy)

    own_copy(0).start()
    for j in range(blocks):
        weight_copy(j).start()
    own_copy(1).start()
    down_copy.start()

    barrier = pltpu.get_barrier_semaphore()
    peers = (partner, y_near, y_far, cross) + x_side + z_side
    for peer in peers:
        pl.semaphore_signal(barrier, inc=1, device_id=peer, device_id_type=MESH)
    pl.semaphore_wait(barrier, len(peers))

    def tok_pair(q):
        lp = (1 - l) if q == 0 else l
        return remote(tok.at[:, lp], X.at[1, :, lp], tk_s.at[q], tk_r.at[q], partner)

    def tok_cross(p):
        return remote(tok.at[p, 1 - l], X.at[2, p, 1 - l], tk_s.at[2 + p], tk_r.at[2 + p], cross)

    def tok_cross_in(p):
        return remote(X.at[2, p, l], X.at[2, p, l], tk_s.at[2 + p], tk_r.at[2 + p], cross)

    def tok_relay(p):
        return remote(X.at[2, p, l], X.at[2, p, l], tk_s.at[6 + p], tk_r.at[6 + p], y_near)

    def tok_relay_in(p):
        return remote(X.at[2, p, 1 - l], X.at[2, p, 1 - l], tk_s.at[6 + p], tk_r.at[6 + p], y_near)

    def tok_forward(q, p):
        lp = l if q == 0 else 1 - l
        i = 10 + 4 * q + p
        return remote(X.at[2, p, lp], X.at[3, p, lp], tk_s.at[i], tk_r.at[i], partner)

    def tok_forward_in(q, p):
        lp = l if q == 0 else 1 - l
        i = 10 + 4 * q + p
        return remote(X.at[3, p, lp], X.at[3, p, lp], tk_s.at[i], tk_r.at[i], partner)

    go(tok_pair(0))
    for p in range(NX):
        go(tok_cross(p))
    go(tok_pair(1))

    def cross_piece(p):
        tok_cross_in(p).wait_recv()
        go(tok_forward(0, p))
        go(tok_relay(p))

    def relay_piece(p):
        tok_relay_in(p).wait_recv()
        go(tok_forward(1, p))

    def rows_ready(u):
        if u in (0, 3):
            q = 0 if u == 0 else 1
            own_copy(q).wait()
            tok_pair(q).wait_recv()
        else:
            for p in range(NX):
                tok_forward_in(u - 1, p).wait_recv()

    def flatten(j):
        weight_copy(j).wait()
        depth = flat.shape[0] // 2

        def piece(i, carry):
            k = pl.multiple_of(i * depth, depth)
            flat[...] = raw[j, pl.ds(k, depth)].reshape(2 * depth, LANES).astype(F32)
            W[j, pl.ds(k, depth), 0:LANES] = flat[pl.ds(0, depth, stride=2), :].astype(BF16)
            W[j, pl.ds(k, depth), LANES:] = flat[pl.ds(1, depth, stride=2), :].astype(BF16)
            return carry

        lax.fori_loop(0, W.shape[1] // depth, piece, 0)

    def project(u, j0, j1):
        hb, lp = unit_half[u]

        def block(j, carry):
            rows = X[2 * hb:2 * hb + 2, :, lp].reshape(NZ * ROWS, X.shape[-1])
            sums = jnp.dot(rows, W[j], preferred_element_type=F32)
            columns = pl.ds(pl.multiple_of(j * 2 * LANES, 2 * LANES), 2 * LANES)
            PS[u, :, :, columns] = sums.reshape(NZ, ROWS, 2 * LANES)
            return carry

        lax.fori_loop(j0, j1, block, 0)

    def hops(g, d):
        return 4 if g % 2 == d else 3

    def slot(g, d, k):
        return k if g % 2 == d else 4 + k

    def step(d, k):
        return k if d == 0 else -k

    def around(d, k):
        return lax.rem(z + step(d, k) + NZ, NZ)

    def sum_table(v, g, d):
        n = hops(g, d)
        if not LONG[v][0]:
            return [(n - k, k - 1 if k else None, 1) for k in range(n)]
        if n == 4:
            return [(4, None, 1), (2, None, 1), (3, 0, 3), (1, 1, 1)]
        return [(3, None, 1), (1, None, 1), (2, 0, 2)]

    def hidden_table(v, g, d):
        n = hops(g, d)
        if not LONG[v][1]:
            return [(k, k - 1 if k else None, 1) for k in range(n)]
        if n == 4:
            return [(0, None, 1), (0, None, 3), (1, 0, 1), (3, 1, 1)]
        return [(0, None, 1), (0, None, 2), (2, 1, 1)]

    def z_peer(d, far):
        return (inp, dep, around(d, far))

    def sums_at(v, g):
        u, r0, r1 = STAGES[v]
        lo = first[g] * 2 * LANES
        return u, slice(r0, r1), slice(lo, lo + GROUPS[g] * 2 * LANES)

    def z_copy(v, g, d, k):
        u, rows, columns = sums_at(v, g)
        i = 7 * g + slot(g, d, k)
        at = (u, slot(g, d, k), rows, columns)
        return remote(S.at[at], R.at[at], rs_s.at[v, i], rs_r.at[v, i], z_peer(d, sum_table(v, g, d)[k][2]))

    def sum_send(v, g, d, k):
        u, rows, columns = sums_at(v, g)
        owner, after, far = sum_table(v, g, d)[k]
        t = PS[u, around(d, owner), rows, columns]
        if after is not None:
            z_copy(v, g, d, after).wait_recv()
            t = t + decode(R[u, slot(g, d, after), rows, columns])
        S[u, slot(g, d, k), rows, columns] = encode(t)
        go(z_copy(v, g, d, k))

    def sum_last(v, g):
        u, rows, columns = sums_at(v, g)
        t = PS[u, z, rows, columns]
        for d in (0, 1):
            for k, (owner, after, far) in enumerate(sum_table(v, g, d)):
                if owner == far:
                    z_copy(v, g, d, k).wait_recv()
                    t = t + decode(R[u, slot(g, d, k), rows, columns])
        for b in range(GROUPS[g]):
            gate = t[:, 2 * b * LANES:(2 * b + 1) * LANES]
            up = t[:, (2 * b + 1) * LANES:(2 * b + 2) * LANES]
            lo = (first[g] + b) * LANES
            H[u, z, rows, lo:lo + LANES] = (gate / (1 + jnp.exp(-gate)) * up).astype(BF16)

    def h_copy(v, g, d, k, o):
        u, r0, r1 = STAGES[v]
        i = 7 * g + slot(g, d, k)
        ref = H.at[u, o, r0:r1, first[g] * LANES:(first[g] + GROUPS[g]) * LANES]
        return remote(ref, ref, ag_s.at[v, i], ag_r.at[v, i], z_peer(d, hidden_table(v, g, d)[k][2]))

    def h_wait(v, g, d, k):
        origin, after, far = hidden_table(v, g, d)[k]
        h_copy(v, g, d, k, around(d, -(origin + far))).wait_recv()

    def h_send(v, g, d, k):
        origin, after, far = hidden_table(v, g, d)[k]
        if after is not None:
            h_wait(v, g, d, after)
        go(h_copy(v, g, d, k, around(d, -origin)))

    def pair_copy(v, b):
        u, r0, r1 = STAGES[v]
        at = (u, b, slice(None), slice(r0, r1))
        return remote(pair_out.at[at], pair_in.at[at], pr_s.at[v, b], pr_r.at[v, b], partner)

    def project_down(v, b):
        u, r0, r1 = STAGES[v]
        if b == 0:
            for g in range(len(GROUPS)):
                for d in (0, 1):
                    for k in range(hops(g, d)):
                        if all(after != k for origin, after, far in hidden_table(v, g, d)):
                            h_wait(v, g, d, k)

        def block(i, carry):
            at = pl.multiple_of(i * 2 * LANES, 2 * LANES)
            rows = H[u, :, r0:r1, :].reshape(NZ * (r1 - r0), H.shape[-1])
            t = jnp.dot(rows, D[:, pl.ds(b * part + at, 2 * LANES)], preferred_element_type=F32)
            t = t.reshape(2, NX, r1 - r0, 2 * LANES)
            own[v % 2, b, :, r0:r1, pl.ds(at, 2 * LANES)] = t[0]
            pair_out[u, b, :, r0:r1, pl.ds(at, 2 * LANES)] = t[1].astype(BF16)
            return carry

        lax.fori_loop(0, part // (2 * LANES), block, 0)
        go(pair_copy(v, b))

    def x_copy(v, b, i):
        u, r0, r1 = STAGES[v]
        d = b % 2 if i != 1 else 1 - b % 2
        at = (u, 3 * b + i, slice(r0, r1))
        return remote(xs.at[at], xr.at[at], x_s.at[v, 3 * b + i], x_r.at[v, 3 * b + i], x_side[d])

    def piece(v, b, k):
        u, r0, r1 = STAGES[v]
        p = lax.rem(x + k + NX, NX)
        return own[v % 2, b, p, r0:r1] + pair_in[u, b, p, r0:r1].astype(F32)

    def x_first(v, b):
        u, r0, r1 = STAGES[v]
        pair_copy(v, b).wait_recv()
        for i, k in ((0, 2), (1, step(b % 2, -1))):
            xs[u, 3 * b + i, r0:r1] = piece(v, b, k).astype(BF16)
            go(x_copy(v, b, i))

    def x_second(v, b):
        u, r0, r1 = STAGES[v]
        x_copy(v, b, 0).wait_recv()
        t = piece(v, b, step(b % 2, 1)) + xr[u, 3 * b, r0:r1].astype(F32)
        xs[u, 3 * b + 2, r0:r1] = t.astype(BF16)
        go(x_copy(v, b, 2))

    def y_copy(v, b):
        u, r0, r1 = STAGES[v]
        return remote(
            ys.at[u, b, r0:r1], yr.at[u, b, r0:r1], y_s.at[v, b], y_r.at[v, b], unit_target[u]
        )

    arrived = set()

    def x_last(v, b):
        u, r0, r1 = STAGES[v]
        t = piece(v, b, 0)
        for i in (1, 2):
            x_copy(v, b, i).wait_recv()
            t = t + xr[u, 3 * b + i, r0:r1].astype(F32)
        if u < UNITS - 1:
            ys[u, b, r0:r1] = t.astype(BF16)
            go(y_copy(v, b))
            return
        if b not in arrived:
            arrived.add(b)
            for other in range(len(STAGES)):
                if STAGES[other][0] < UNITS - 1:
                    y_copy(other, b).wait_recv()
        for other in range(UNITS - 1):
            t = t + yr[other, b, r0:r1].astype(F32)
        out[r0:r1, b * part:(b + 1) * part] = t.astype(BF16)

    steps = {
        CROSS: cross_piece, RELAY: relay_piece, WEIGHT: flatten, SUM: sum_send, END: sum_last, HIDDEN: h_send,
        DOWN: project_down, X1: x_first, X2: x_second, X3: x_last,
    }
    ready, fetched, i = set(), False, 0
    while i < len(ORDER):
        kind, *at = ORDER[i]
        i += 1
        if kind == PRODUCT:
            u, j = at
            if u not in ready:
                ready.add(u)
                rows_ready(u)
            end = j + 1
            while i < len(ORDER) and ORDER[i] == (PRODUCT, u, end):
                end, i = end + 1, i + 1
            project(u, j, end)
            continue
        if kind == DOWN and not fetched:
            fetched = True
            down_copy.wait()
        steps[kind](*at)

    for copy in started:
        copy.wait_send()


def shards(tokens, gate_up_weight, down_weight):
    width = tokens.shape[1]
    units = gate_up_weight.shape[2]
    blocks = units // LANES
    part = width // PARTS
    stages, links = len(STAGES), 7 * len(GROUPS)
    dma = pltpu.SemaphoreType.DMA
    any_space = pl.BlockSpec(memory_space=pl.ANY)
    vmem = pltpu.VMEM
    return pl.pallas_call(
        kernel,
        out_shape=jax.ShapeDtypeStruct((ROWS, width), BF16),
        in_specs=[any_space] * 3,
        out_specs=pl.BlockSpec(memory_space=pltpu.VMEM),
        scratch_shapes=[
            vmem((4, NX, 2, ROWS, width), BF16),
            vmem((blocks, width, 2, LANES), BF16),
            vmem((512, LANES), F32),
            vmem((blocks, width, 2 * LANES), BF16),
            vmem((units, width), BF16),
            vmem((UNITS, NZ, ROWS, 2 * units), F32),
            vmem((UNITS, 7, ROWS, 2 * units), BF16),
            vmem((UNITS, 7, ROWS, 2 * units), BF16),
            vmem((UNITS, NZ, ROWS, units), BF16),
            vmem((2, PARTS, NX, ROWS, part), F32),
            vmem((UNITS, PARTS, NX, ROWS, part), BF16),
            vmem((UNITS, PARTS, NX, ROWS, part), BF16),
            vmem((UNITS, 3 * PARTS, ROWS, part), BF16),
            vmem((UNITS, 3 * PARTS, ROWS, part), BF16),
            vmem((UNITS - 1, PARTS, ROWS, part), BF16),
            vmem((UNITS - 1, PARTS, ROWS, part), BF16),
            dma((3,)),
            dma((blocks,)),
            dma((18,)),
            dma((18,)),
            dma((stages, links)),
            dma((stages, links)),
            dma((stages, links)),
            dma((stages, links)),
            dma((stages, PARTS)),
            dma((stages, PARTS)),
            dma((stages, 3 * PARTS)),
            dma((stages, 3 * PARTS)),
            dma((stages, PARTS)),
            dma((stages, PARTS)),
        ],
        compiler_params=pltpu.CompilerParams(
            collective_id=0, has_side_effects=True, vmem_limit_bytes=62 << 20
        ),
    )(tokens.reshape(NX, 2, ROWS, width), gate_up_weight, down_weight)


def solution(mesh):
    placed = (P("inp", "out"), P("out", None, ("inp", "dep")), P(("inp", "dep"), "out"))
    return jax.shard_map(
        shards, mesh=mesh, in_specs=placed, out_specs=P(("inp", "dep"), "out"), check_vma=False
    )
```

time: 444 us -> 94.8 us (0.21)
  waiting for transfers between devices: 383 us -> 0 us
  Pallas kernels: 0 us -> 93.1 us
  matrix products: 26.2 us -> 0 us
  local copies, waits for them, and re-layouts: 18.1 us -> 1.57 us
  between operations: 13.1 us -> 0.01 us
    reduce_scatter x1 -> x0, waiting for transfers between devices: 185 us -> none  [shards(): lax.psum_scatter(jnp.dot(full_hidden, down_weight, preferred_element_type...]
    psum x1 -> x0, waiting for transfers between devices: 167 us -> none  [shards(): totals = lax.psum(projected, 'out')]
    pallas_call x0 -> x1, Pallas kernels: none -> 93.1 us  [shards(): pl.pallas_call(kernel, out_shape=jax.ShapeDtypeStruct((ROWS, width), BF16...]
    all_gather x1 -> x0, waiting for transfers between devices: 29.1 us -> none  [shards(): lax.all_gather(tokens, 'inp', axis=0, tiled=True)]
    dot_general x2 -> x0, matrix products: 26.2 us -> none  [the longest x1 14.3 us: shards(): jnp.dot(lax.all_gather(tokens, 'inp', axis=0, tiled=True), flat_weight, p...]
    dot_general x1 -> x0, local copies, waits for them, and re-layouts: 10.5 us -> none  [shards(): jnp.dot(lax.all_gather(tokens, 'inp', axis=0, tiled=True), flat_weight, p...]
    unnamed x1, local copies, waits for them, and re-layouts: 7.6 us -> 1.57 us
  transfers between devices with their start and end apart: 3 -> 0, of which waited for: 3 -> 0; matrix products, arithmetic and copies ran while one was open for 4% -> 0% of each run, Pallas kernels for 0% -> 0%
where the time goes in v2:
time: 94.8 us; the launch traced here: 94.7 us
  Pallas kernels  93.1 us (98%)
  local copies, waits for them, and re-layouts  1.57 us (2%)
    pallas_call x1, Pallas kernels, shards(): pl.pallas_call(kernel, out_shape=jax.ShapeDtypeStruct((ROWS, width), BF16...  93.1 us

profile of v2, /device:TPU:1, one launch (start us, length us, event | category | flops | bytes accessed | tf_op | source)
XLA Modules:
  0.0 94.7 jit_solution(65744234638643799)
XLA Ops:
  0.0 93.1 %shard_map.37 = bf16[32,2048]{1,0:T(8,128)(2,1)} custom-call(bf16[4,2,32,2048]{3,2,1,0:T(8,128)(2,1)} %bitcast.1, bf16[2048,2,896]{2,1,0:T(2,128)(2,1)} %gate_up.1, bf16[896,2048]{1,0:T(8,128)(2,1)} %down.1), custom_call_target="tpu_custom_call" | custom-call | tf_op jit(solution)/shard_map/pallas_call | solution.py:391
  93.1 1.6 %copy.5 = bf16[32,2048]{1,0:T(8,128)(2,1)} copy(bf16[32,2048]{1,0:T(8,128)(2,1)} %shard_map.37) | data formatting | bytes 262144

commit v3 on v2

--- a/solution.py
+++ b/solution.py
@@ -14,6 +14,7 @@
 PARTS = 4
 LONG = ((False, False), (False, False), (False, False), (False, True))
 CROSS, RELAY, WEIGHT, PRODUCT, SUM, END, HIDDEN, DOWN, X1, X2, X3 = range(11)
+AHEAD = 2
 ORDER = (
     (WEIGHT, 0), (WEIGHT, 1), (WEIGHT, 2), (WEIGHT, 3), (PRODUCT, 3, 0), (PRODUCT, 3, 1), (PRODUCT, 3, 2), (PRODUCT, 3, 3),
     (SUM, 3, 0, 0, 0), (SUM, 3, 0, 1, 0), (PRODUCT, 0, 0), (PRODUCT, 0, 1), (PRODUCT, 0, 2), (PRODUCT, 0, 3),
@@ -106,17 +107,16 @@
         copy.start()
         started.append(copy)
 
-    own_copy(0).start()
     for j in range(blocks):
         weight_copy(j).start()
-    own_copy(1).start()
+        if j < 2:
+            own_copy(1 - j).start()
     down_copy.start()
 
     barrier = pltpu.get_barrier_semaphore()
     peers = (partner, y_near, y_far, cross) + x_side + z_side
     for peer in peers:
         pl.semaphore_signal(barrier, inc=1, device_id=peer, device_id_type=MESH)
-    pl.semaphore_wait(barrier, len(peers))
 
     def tok_pair(q):
         lp = (1 - l) if q == 0 else l
@@ -143,11 +143,6 @@
         lp = l if q == 0 else 1 - l
         i = 10 + 4 * q + p
         return remote(X.at[3, p, lp], X.at[3, p, lp], tk_s.at[i], tk_r.at[i], partner)
-
-    go(tok_pair(0))
-    for p in range(NX):
-        go(tok_cross(p))
-    go(tok_pair(1))
 
     def cross_piece(p):
         tok_cross_in(p).wait_recv()
@@ -179,6 +174,15 @@
             return carry
 
         lax.fori_loop(0, W.shape[1] // depth, piece, 0)
+
+    early = [at[0] for kind, *at in ORDER[:AHEAD]]
+    for j in early:
+        flatten(j)
+    pl.semaphore_wait(barrier, len(peers))
+    for p in range(NX):
+        go(tok_cross(p))
+    for q in (1, 0):
+        go(tok_pair(q))
 
     def project(u, j0, j1):
         hb, lp = unit_half[u]
@@ -356,7 +360,7 @@
         CROSS: cross_piece, RELAY: relay_piece, WEIGHT: flatten, SUM: sum_send, END: sum_last, HIDDEN: h_send,
         DOWN: project_down, X1: x_first, X2: x_second, X3: x_last,
     }
-    ready, fetched, i = set(), False, 0
+    ready, fetched, i = set(), False, AHEAD
     while i < len(ORDER):
         kind, *at = ORDER[i]
         i += 1

time: 94.8 us -> 94.8 us (level)
  no operation moved by 1% of the time
where the time goes in v3:
time: 94.8 us; the launch traced here: 94.2 us
  Pallas kernels  92.6 us (98%)
  local copies, waits for them, and re-layouts  1.57 us (2%)
    pallas_call x1, Pallas kernels, shards(): pl.pallas_call(kernel, out_shape=jax.ShapeDtypeStruct((ROWS, width), BF16...  92.6 us

profile of v3, /device:TPU:1, one launch (start us, length us, event | category | flops | bytes accessed | tf_op | source)
XLA Modules:
  0.0 94.2 jit_solution(238213221384590028)
XLA Ops:
  0.0 92.6 %shard_map.37 = bf16[32,2048]{1,0:T(8,128)(2,1)} custom-call(bf16[4,2,32,2048]{3,2,1,0:T(8,128)(2,1)} %bitcast.1, bf16[2048,2,896]{2,1,0:T(2,128)(2,1)} %gate_up.1, bf16[896,2048]{1,0:T(8,128)(2,1)} %down.1), custom_call_target="tpu_custom_call" | custom-call | tf_op jit(solution)/shard_map/pallas_call | solution.py:395
  92.6 1.6 %copy.5 = bf16[32,2048]{1,0:T(8,128)(2,1)} copy(bf16[32,2048]{1,0:T(8,128)(2,1)} %shard_map.37) | data formatting | bytes 262144
